TPU v7x, 512 devices: a whole 4x8x8 slice. The times are simulated.
512 devices in a mesh: seq: 64 (over y, z), head: 8 (over x, core).
Axes of the slice: x: 4, y: 8, z: 8, core: 2. Of those that a mesh axis runs over, the one named last changes fastest.
Arguments:
- layer_input_rows: bfloat16 [8192, 4096], P('seq', 'head'), may hold values from -6 to 6
- filter_input_channels: bfloat16 [8192, 8192], P('seq', 'head'), may hold values from -6 to 6
- gate_input_channels: bfloat16 [8192, 8192], P('seq', 'head'), may hold values from -6 to 6
- state_input_vectors: bfloat16 [8192, 128], P('seq'), may hold values from -3 to 3
- state_output_vectors: bfloat16 [8192, 128], P('seq'), may hold values from -3 to 3
- decay_logarithm: float32 [8192, 64], P('seq', 'head'), may hold values from -0.7 to 0, as said below
- filter_tap_weight: bfloat16 [4, 8192], P(None, 'head'), may hold values from -3 to 3
- head_skip_gain: float32 [64], P('head'), may hold values from 0.5 to 1.5
- gated_norm_gain: float32 [8192], P('head'), may hold values from 0.1 to 1.9
- adapter_down_in: bfloat16 [4096, 32], P('head'), may hold values from -0.09375 to 0.09375
- adapter_up_in: bfloat16 [2, 32, 8192], P(None, None, 'head'), may hold values from -1 to 1
- adapter_down_out: bfloat16 [8192, 32], P('head'), may hold values from -0.0625 to 0.0625
- adapter_up_out: bfloat16 [32, 4096], P(None, 'head'), may hold values from -1 to 1
- output_gradient: bfloat16 [8192, 4096], P('seq', 'head'), may hold values from -6 to 6
- base_path_gradient: bfloat16 [8192, 8192], P('seq', 'head'), may hold values from -6 to 6
Outputs:
- grad_conv_in: bfloat16 [8192, 8192], P('seq', 'head')
- grad_gate_in: bfloat16 [8192, 8192], P('seq', 'head')
- grad_state_b: float32 [8192, 128], P(('seq', 'head'))
- grad_state_c: float32 [8192, 128], P(('seq', 'head'))
- grad_log_decay: float32 [8192, 64], P('seq', 'head')
- grad_layer_in: bfloat16 [8192, 4096], P('seq', 'head')
- grad_lora_a_in: float32 [4096, 32], P('head')
- grad_lora_b_in: float32 [2, 32, 8192], P(None, None, 'head')
- grad_lora_a_out: float32 [8192, 32], P('head')
- grad_lora_b_out: float32 [32, 4096], P(None, 'head')
Inputs may be any that keep to these rules, and one draw needn't show every extreme that they name: `decay_logarithm`: each entry is the logarithm of a decay factor between 0 and 1.
All inputs are finite; a program needn't handle non-finite values.
Results may differ from a plain program's by a relative error of at most 0.0017.
Values may be sent and summed in bfloat16 or wider, within the bound.
A program may use at most 128 MiB of HBM per device.

v0:
```python
import jax
import jax.numpy as jnp
from jax import lax
from jax.sharding import PartitionSpec as P

HDIM = 128
NSTATE = 128
BLOCK = 256
PRECISE_PRODUCT = lax.Precision.HIGHEST
ADAPTER_SCALE = 2.0
NORM_EPS = 1e-05


def passed_along(x, axis, by):
    devices = lax.axis_size(axis)
    pairs = [(i, i + by) for i in range(devices) if 0 <= i + by < devices]
    return lax.ppermute(x, axis, pairs)


def prefix(part, axis, combine, identity, reverse):
    count = lax.axis_size(axis)
    place = lax.axis_index(axis)
    ahead = count - 1 - place if reverse else place
    gathered = jax.tree.map(lambda a: lax.all_gather(a, axis), part)
    state = jax.tree.map(lambda a, e: jnp.zeros_like(a) + jnp.asarray(e, a.dtype), part, identity)

    def one(turn, state):
        source = count - 1 - turn if reverse else turn
        return combine(
            state, jax.tree.map(lambda a: lax.dynamic_index_in_dim(a, source, 0, False), gathered)
        )

    return lax.fori_loop(0, ahead, one, state)


def block_pass(activated, b_float, c_float, logarithm_increments, start_state, block_rows):
    tok_rows, head_count, head_width = activated.shape
    block_count = tok_rows // block_rows
    state_width = b_float.shape[1]
    causal = (jnp.arange(block_rows)[:, None] >= jnp.arange(block_rows)[None, :])[None, :, :]

    def advance(carried_state, block_items):
        x_block, b_block, c_block, l_block = block_items
        cum_decay = jnp.cumsum(l_block, axis=0)
        cum_heads = cum_decay.T
        decay_gap = jnp.where(causal, cum_heads[:, :, None] - cum_heads[:, None, :], 0.0)
        decays = jnp.where(causal, jnp.exp(decay_gap), 0.0)
        scores = jnp.dot(c_block, b_block.T, precision=PRECISE_PRODUCT)
        weights = decays * scores[None, :, :]
        inner_out = jnp.einsum("hts,shp->thp", weights, x_block, precision=PRECISE_PRODUCT)
        outer_out = jnp.exp(cum_decay)[:, :, None] * jnp.einsum(
            "tn,hnp->thp", c_block, carried_state, precision=PRECISE_PRODUCT
        )
        to_end = jnp.exp(cum_decay[-1][None, :] - cum_decay)
        fresh_state = jnp.einsum(
            "sn,shp->hnp", b_block, x_block * to_end[:, :, None], precision=PRECISE_PRODUCT
        )
        next_state = jnp.exp(cum_decay[-1])[:, None, None] * carried_state + fresh_state
        return (next_state, inner_out + outer_out)

    block_items = (
        activated.reshape(block_count, block_rows, head_count, head_width),
        b_float.reshape(block_count, block_rows, state_width),
        c_float.reshape(block_count, block_rows, state_width),
        logarithm_increments.reshape(block_count, block_rows, head_count),
    )
    end_state, outputs = lax.scan(advance, start_state, block_items)
    return (outputs.reshape(tok_rows, head_count, head_width), end_state)


def carried(c_float, logarithm_increments, state_in):
    cum_decay = jnp.cumsum(logarithm_increments, axis=0)
    outer_out = jnp.exp(cum_decay)[:, :, None] * jnp.einsum(
        "tn,hnp->thp", c_float, state_in, precision=PRECISE_PRODUCT
    )
    passed = jnp.exp(cum_decay[-1])[:, None, None] * state_in
    return (outer_out, passed)


def end_state(activated, b_float, logarithm_increments):
    cum_decay = jnp.cumsum(logarithm_increments, axis=0)
    to_end = jnp.exp(cum_decay[-1][None, :] - cum_decay)
    return jnp.einsum(
        "sn,shp->hnp", b_float, activated * to_end[:, :, None], precision=PRECISE_PRODUCT
    )


def chain_step(earlier, later_part):
    return (
        earlier[0] + later_part[0],
        jnp.exp(later_part[0])[:, None, None] * earlier[1] + later_part[1],
    )


def body(
    layer_input_rows,
    filter_input_channels,
    gate_input_channels,
    state_input_vectors,
    state_output_vectors,
    decay_logarithm,
    filter_tap_weight,
    head_skip_gain,
    gated_norm_gain,
    adapter_down_in,
    adapter_up_in,
    adapter_down_out,
    adapter_up_out,
    output_gradient,
    base_path_gradient,
):
    tok_rows, chan_width = filter_input_channels.shape
    head_count = decay_logarithm.shape[1]
    rim_rows = filter_tap_weight.shape[0] - 1
    block_rows = min(BLOCK, tok_rows)
    row_total_count = tok_rows * lax.axis_size("seq")
    all_channels = chan_width * lax.axis_size("head")
    taps = filter_tap_weight.astype(jnp.float32)
    before = passed_along(filter_input_channels[tok_rows - rim_rows :], "seq", 1)
    padded = jnp.concatenate([before, filter_input_channels], axis=0).astype(jnp.float32)
    pre_act = padded[0:tok_rows] * taps[0][None, :]
    for offset in range(1, rim_rows + 1):
        pre_act = pre_act + padded[offset : offset + tok_rows] * taps[offset][None, :]
    act_heads = jax.nn.silu(pre_act).reshape(tok_rows, head_count, HDIM)
    b_float = state_input_vectors.astype(jnp.float32)
    c_float = state_output_vectors.astype(jnp.float32)
    zero_state = jnp.zeros((head_count, NSTATE, HDIM), jnp.float32)
    zero_decay = jnp.zeros((head_count,), jnp.float32)

    def local_pass(activated, b_part, c_part, logarithm_increments):
        return block_pass(activated, b_part, c_part, logarithm_increments, zero_state, block_rows)

    (inner_out, fresh_state), pull_local = jax.vjp(
        local_pass, act_heads, b_float, c_float, decay_logarithm
    )
    total_decay = jnp.sum(decay_logarithm, axis=0)
    _, state_in = prefix(
        (total_decay, fresh_state), "seq", chain_step, (zero_decay, zero_state), False
    )
    (outer_out, _), pull_carry = jax.vjp(carried, c_float, decay_logarithm, state_in)
    ssd_out = inner_out + outer_out + head_skip_gain[None, :, None] * act_heads
    mixer_out = ssd_out.reshape(tok_rows, chan_width)
    gate_float = gate_input_channels.astype(jnp.float32)
    gate_sig = jax.nn.sigmoid(gate_float)
    gated_out = mixer_out * gate_float * gate_sig
    square_part = jnp.sum(gated_out * gated_out, axis=1)
    scaled = gated_out * gated_norm_gain[None, :]
    down_out_factor = adapter_down_out.astype(jnp.float32)
    square_sum = lax.psum(square_part, "head")
    inv_rms = lax.rsqrt(square_sum / all_channels + NORM_EPS)
    normed = scaled * inv_rms[:, None]
    low_out = lax.psum(jnp.dot(normed, down_out_factor, precision=PRECISE_PRODUCT), "head")
    reverse_out_grad = lax.psum(
        jnp.dot(output_gradient, adapter_up_out.T, preferred_element_type=jnp.float32), "head"
    )
    normalized_gradient = base_path_gradient.astype(jnp.float32) + ADAPTER_SCALE * jnp.dot(
        reverse_out_grad, down_out_factor.T, precision=PRECISE_PRODUCT
    )
    weighted = normalized_gradient * gated_norm_gain[None, :]
    dot_total = lax.psum(jnp.sum(weighted * gated_out, axis=1), "head")
    grad_gated = (
        inv_rms[:, None] * weighted
        - gated_out * (inv_rms * inv_rms * inv_rms * dot_total / all_channels)[:, None]
    )
    grad_mixer = grad_gated * gate_float * gate_sig
    grad_gate = grad_gated * mixer_out * gate_sig * (1.0 + gate_float * (1.0 - gate_sig))
    grad_ssd = grad_mixer.reshape(tok_rows, head_count, HDIM)
    cum_decay = jnp.cumsum(decay_logarithm, axis=0)
    local_grad = jnp.einsum(
        "tn,thp->hnp", c_float, grad_ssd * jnp.exp(cum_decay)[:, :, None], precision=PRECISE_PRODUCT
    )
    _, state_grad = prefix(
        (total_decay, local_grad), "seq", chain_step, (zero_decay, zero_state), True
    )
    grad_act, grad_b, grad_c, grad_steps = pull_local((grad_ssd, state_grad))
    carry_c, carry_steps, _ = pull_carry((grad_ssd, state_grad))
    grad_c = grad_c + carry_c
    grad_steps = grad_steps + carry_steps
    grad_act = grad_act + head_skip_gain[None, :, None] * grad_ssd
    pre_sig = jax.nn.sigmoid(pre_act)
    grad_pre = grad_act.reshape(tok_rows, chan_width) * pre_sig * (1.0 + pre_act * (1.0 - pre_sig))
    after = passed_along(grad_pre[:rim_rows], "seq", -1)
    extended = jnp.concatenate([grad_pre, after], axis=0)
    grad_conv = extended[rim_rows : rim_rows + tok_rows] * taps[0][None, :]
    for offset in range(1, rim_rows + 1):
        grad_conv = (
            grad_conv
            + extended[rim_rows - offset : rim_rows - offset + tok_rows] * taps[offset][None, :]
        )
    grad_b_rows, grad_c_rows = (
        lax.psum_scatter(grad_b, "head", scatter_dimension=0, tiled=True),
        lax.psum_scatter(grad_c, "head", scatter_dimension=0, tiled=True),
    )
    reduced_input = lax.psum(
        jnp.dot(layer_input_rows, adapter_down_in, preferred_element_type=jnp.float32), "head"
    )
    up_in_factor = adapter_up_in.astype(jnp.float32)
    back_part = jnp.dot(grad_conv, up_in_factor[0].T, precision=PRECISE_PRODUCT) + jnp.dot(
        grad_gate, up_in_factor[1].T, precision=PRECISE_PRODUCT
    )
    reverse_in_grad = lax.psum(back_part, "head")
    layer_gradient_fn = (
        ADAPTER_SCALE
        * jnp.dot(reverse_in_grad, adapter_down_in.astype(jnp.float32).T, precision=PRECISE_PRODUCT)
    ).astype(jnp.bfloat16)
    averaging_scale = ADAPTER_SCALE / row_total_count
    grad_a_in, grad_b_in, grad_a_out, grad_b_out = lax.psum(
        (
            averaging_scale
            * jnp.dot(
                layer_input_rows.astype(jnp.float32).T, reverse_in_grad, precision=PRECISE_PRODUCT
            ),
            averaging_scale
            * jnp.stack(
                [
                    jnp.dot(reduced_input.T, grad_conv, precision=PRECISE_PRODUCT),
                    jnp.dot(reduced_input.T, grad_gate, precision=PRECISE_PRODUCT),
                ]
            ),
            averaging_scale * jnp.dot(normed.T, reverse_out_grad, precision=PRECISE_PRODUCT),
            averaging_scale
            * jnp.dot(low_out.T, output_gradient.astype(jnp.float32), precision=PRECISE_PRODUCT),
        ),
        "seq",
    )
    return (
        grad_conv.astype(jnp.bfloat16),
        grad_gate.astype(jnp.bfloat16),
        grad_b_rows,
        grad_c_rows,
        grad_steps,
        layer_gradient_fn,
        grad_a_in,
        grad_b_in,
        grad_a_out,
        grad_b_out,
    )


def solution(mesh):
    in_specs = (
        P("seq", "head"),
        P("seq", "head"),
        P("seq", "head"),
        P("seq", None),
        P("seq", None),
        P("seq", "head"),
        P(None, "head"),
        P("head"),
        P("head"),
        P("head", None),
        P(None, None, "head"),
        P("head", None),
        P(None, "head"),
        P("seq", "head"),
        P("seq", "head"),
    )
    out_specs = (
        P("seq", "head"),
        P("seq", "head"),
        P(("seq", "head"), None),
        P(("seq", "head"), None),
        P("seq", "head"),
        P("seq", "head"),
        P("head", None),
        P(None, None, "head"),
        P("head", None),
        P(None, "head"),
    )
    return jax.shard_map(body, mesh=mesh, in_specs=in_specs, out_specs=out_specs, check_vma=False)
```

profile of v0, /device:TPU:2, one launch (start us, length us, event | category | flops | bytes accessed | tf_op | source)
XLA Modules:
  0.0 900.4 jit_solution(9360454591310786965)
XLA Ops:
  8.1 4.3 collective-permute-start
  19.9 1.3 dynamic-slice
  22.1 151.3 %all-reduce.3 = f32[512]{0:T(512)S(1)} all-reduce(f32[512]{0:T(512)S(1)} %dynamic-update-slice), channel_id=2, replica_groups=mesh['seq'=64,'head'=8] {'seq'}, use_global_device_ids=true, to_apply=%add.3 | all-reduce | flops 512 | bytes 4096
  175.6 21.8 %psum.71 = f32[128,32]{0,1:T(8,128)} all-reduce(f32[128,32]{0,1:T(8,128)S(1)} %fusion.89), channel_id=1, replica_groups=mesh['seq'=64,'head'=8] {'head'}, use_global_device_ids=true, to_apply=%region_6.7 | all-reduce | flops 4096 | bytes 32768 | tf_op jit(solution)/shard_map/psum | solution.py:153
  199.4 48.0 %all-gather.6.cloned.1.call-done = f32[512,128,128]{2,1,0:T(8,128)} async-done(((f32[8,128,128]{2,1,0:T(8,128)}), f32[512,128,128]{2,1,0:T(8,128)}) %all-gather.6.cloned.1.call-update) | async-done | bytes 33554448 | tf_op jit(solution)/shard_map/all_gather | solution.py:24
  248.1 1.3 convolution_bitcast_fusion.2
  249.4 2.1 fusion.6
  251.8 3.2 multiply_reduce_fusion.7
  254.9 12.4 %all-reduce.6 = (f32[128]{0:T(128)}, f32[128]{0:T(128)}) all-reduce(f32[128]{0:T(128)} %get-tuple-element.524, f32[128]{0:T(128)} %get-tuple-element.523), channel_id=1, replica_groups=mesh['seq'=64,'head'=8] {'head'}, use_global_device_ids=true, to_apply=%region_8.9 | all-reduce | flops 256 | bytes 2048 | tf_op jit(solution)/shard_map/psum | solution.py:160
  268.0 2.8 fusion.81
  270.8 1.2 copy.139
  272.0 1.9 convolution_bitcast_fusion.1
  274.0 2.0 copy.140
  276.1 1.3 broadcast_bitcast_fusion
  277.4 1.5 fusion.90
  278.9 1.6 convolution_bitcast_fusion.9
  280.5 1.7 convolution_bitcast_fusion.8
  282.9 2.0 fusion.43
  285.7 1.5 fusion.41
  287.3 2.2 convolution_multiply_fusion.2
  289.6 280.1 %all-gather.8.cloned.1.call-done = f32[512,128,128]{2,1,0:T(8,128)} async-done(((f32[8,128,128]{2,1,0:T(8,128)}), f32[512,128,128]{2,1,0:T(8,128)}) %all-gather.8.cloned.1.call-update) | async-done | bytes 33554448 | tf_op jit(solution)/shard_map/all_gather | solution.py:24
  569.8 120.5 %while.21 = (s32[]{:T(128)}, f32[8,128,128]{2,1,0:T(8,128)S(1)}, s32[]{:T(128)}, f32[64,8]{1,0:T(8,128)}, f32[64,8,128,128]{3,2,1,0:T(8,128)}, /*index=5*/s32[]{:T(128)}, s32[]{:T(128)}, s32[]{:T(128)}, s32[]{:T(128)}) while((s32[]{:T(128)}, f32[8,128,128]{2,1,0:T(8,128)S(1)}, s32[]{:T(128)}, f32[64,8]{1,0:T(8,128)}, ...), condition=%wide.region_10.11_spmd, body=%wide.region_9.10_spmd.sunk | while | flops 262150 | bytes 1573115 | solution.py:33
  570.5 1.2 bitcast_add_fusion.6
  572.4 1.2 bitcast_add_fusion.6
  574.3 1.2 bitcast_add_fusion.6
  576.2 1.2 bitcast_add_fusion.6
  578.1 1.2 bitcast_add_fusion.6
  587.7 1.2 bitcast_add_fusion.6
  589.6 1.2 bitcast_add_fusion.6
  591.5 1.2 bitcast_add_fusion.6
  595.3 1.2 bitcast_add_fusion.6
  597.2 1.2 bitcast_add_fusion.6
  603.0 1.2 bitcast_add_fusion.6
  690.5 1.7 convolution_bitcast_fusion.10
  693.8 1.6 fusion.2
  695.6 1.4 add_multiply_fusion
  697.0 1.3 collective-permute-start.1
  699.2 3.5 collective-permute-done.1
  702.7 1.7 fusion.83
  704.3 1.2 fusion.65
  705.5 1.2 convolution_add_fusion.3
  706.8 21.9 %all-reduce.5 = (f32[128,32]{0,1:T(8,128)S(1)}, f32[128,32]{0,1:T(8,128)S(1)}, f32[128,32]{0,1:T(8,128)S(1)}) all-reduce(f32[128,32]{0,1:T(8,128)S(1)} %convolution_add_fusion.3, f32[128,32]{0,1:T(8,128)} %fusion.90, f32[128,32]{0,1:T(8,128)S(1)} %fusion.41), channel_id=1, replica_groups=mesh['seq'=64,'head'=8] {'head'}, use_global_device_ids=true, to_apply=%region_24.25 | all-reduce | flops 12288 | bytes 98304 | tf_op jit(solution)/shard_map/psum | solution.py:201
  736.6 1.7 fusion.7
  738.4 149.3 %all-reduce.9.cloned.1.call-done = (f32[512,32]{0,1:T(8,128)}, f32[2,32,1024]{2,1,0:T(8,128)}, f32[1024,32]{0,1:T(8,128)}, f32[32,512]{1,0:T(8,128)}) async-done(((f32[512,32]{0,1:T(8,128)}, f32[2,32,1024]{2,1,0:T(8,128)}, f32[1024,32]{0,1:T(8,128)}, f32[32,512]{1,0:T(8,128)}), (f32[512,32]{0,1:T(8,128)}, f32[2,32,1024]{2,1,0:T(8,128)}, f32[1024,32]{0,1:T(8,128)}, ...) | async-done | bytes 524304 | tf_op jit(solution)/shard_map/psum | solution.py:207
  887.7 1.5 copy.191
  889.2 1.7 copy.192
  890.8 1.6 copy.193
  892.4 1.5 copy.194
  (213 shorter events, 132.5 us)
Async XLA Ops:
  7.2 167.5 %copy-start = (bf16[128,512]{1,0:T(8,128)(2,1)S(1)}, bf16[128,512]{1,0:T(8,128)(2,1)}, u32[]{:S(2)}) copy-start(bf16[128,512]{1,0:T(8,128)(2,1)} %param.32) | copy-start | bytes 393220
  7.2 277.7 %copy-start.4 = (bf16[128,128]{1,0:T(8,128)(2,1)S(1)}, bf16[128,128]{1,0:T(8,128)(2,1)}, u32[]{:S(2)}) copy-start(bf16[128,128]{1,0:T(8,128)(2,1)} %param.22) | copy-start | bytes 98308
  7.2 685.7 %copy-start.3 = (bf16[128,128]{1,0:T(8,128)(2,1)S(1)}, bf16[128,128]{1,0:T(8,128)(2,1)}, u32[]{:S(2)}) copy-start(bf16[128,128]{1,0:T(8,128)(2,1)} %param.23) | copy-start | bytes 98308
  7.2 270.2 %copy-start.5 = (bf16[128,512]{1,0:T(8,128)(2,1)S(1)}, bf16[128,512]{1,0:T(8,128)(2,1)}, u32[]{:S(2)}) copy-start(bf16[128,512]{1,0:T(8,128)(2,1)} %param.19) | copy-start | bytes 393220
  7.2 240.2 %all-gather.6.cloned.1.call-start = ((), (), s32[]{:S(2)}) async-start(), calls=%async_computation.4 | async-start | bytes 34078720 | tf_op jit(solution)/shard_map/all_gather | solution.py:24
  8.1 6.5 collective-permute-start
  13.2 3.5 copy-start.10
  13.2 3.5 copy-start.11
  13.2 3.5 copy-start.12
  13.2 3.5 copy-start.13
  14.2 159.3 %copy-start.9 = (f32[128,8]{0,1:T(8,128)}, f32[128,8]{0,1:T(8,128)S(1)}, u32[]{:S(2)}) copy-start(f32[128,8]{0,1:T(8,128)S(1)} %copy.132) | copy-start | bytes 12292
  14.5 182.8 %copy-start.6 = (f32[128,8]{0,1:T(8,128)}, f32[128,8]{0,1:T(8,128)S(1)}, u32[]{:S(2)}) copy-start(f32[128,8]{0,1:T(8,128)S(1)} %get-tuple-element.573) | copy-start | bytes 12292
  14.5 237.0 %copy-start.8 = (f32[128,8]{0,1:T(8,128)}, f32[128,8]{0,1:T(8,128)S(1)}, u32[]{:S(2)}) copy-start(f32[128,8]{0,1:T(8,128)S(1)} %get-tuple-element.574) | copy-start | bytes 12292
  19.1 550.6 %all-gather.8.cloned.1.call-start = ((), (), s32[]{:S(2)}) async-start(), calls=%async_computation.5 | async-start | bytes 34078720 | tf_op jit(solution)/shard_map/all_gather | solution.py:24
  173.6 78.0 %copy-start.7 = (f32[8,128]{1,0:T(8,128)}, f32[8,128]{1,0:T(8,128)S(1)}, u32[]{:S(2)}) copy-start(f32[8,128]{1,0:T(8,128)S(1)} %copy.129) | copy-start | bytes 12292
  247.5 0.6 copy-start.14
  251.7 16.2 %copy-start.2 = (f32[128,1024]{1,0:T(8,128)}, f32[128,1024]{1,0:T(8,128)S(1)}, u32[]{:S(2)}) copy-start(f32[128,1024]{1,0:T(8,128)S(1)} %copy.138) | copy-start | bytes 1572868
  254.9 15.9 %copy-start.1 = (f32[128,1024]{1,0:T(8,128)}, f32[128,1024]{1,0:T(8,128)S(1)}, u32[]{:S(2)}) copy-start(f32[128,1024]{1,0:T(8,128)S(1)} %get-tuple-element.560) | copy-start | bytes 1572868
  268.0 2.8 copy-start.15
  276.0 462.3 %reduce-scatter.5.cloned.1.call-start = ((), (), s32[]{:S(2)}) async-start(), calls=%async_computation.3 | async-start | bytes 73728 | tf_op jit(solution)/shard_map/reduce_scatter | solution.py:192
  289.5 448.9 %reduce-scatter.3.cloned.1.call-start = ((), (), s32[]{:S(2)}) async-start(), calls=%async_computation.2 | async-start | bytes 73728 | tf_op jit(solution)/shard_map/reduce_scatter | solution.py:191
  697.0 5.6 collective-permute-start.1
  699.1 188.6 %all-reduce.9.cloned.1.call-start = ((), (), s32[]{:S(2)}) async-start(), calls=%async_computation.6 | async-start | bytes 1048576 | tf_op jit(solution)/shard_map/psum | solution.py:207
Sparse Core Ops, SparseCore 0:
  19.2 228.1 all-gather.5
  276.1 293.5 all-gather.7
  573.1 30.7 reduce-scatter.4
  699.2 25.5 reduce-scatter.2
  732.0 155.6 all-reduce.8
where the time goes:
time: 907 us; the launch traced here: 900 us
  waiting for transfers between devices  481 us (53%)
  blocking collectives  207 us (23%)
  other arithmetic  90.8 us (10%)
  local copies, waits for them, and re-layouts  63.6 us (7%)
  matrix products  35.3 us (4%)
  between operations  14.8 us (2%)
    all_gather x2, waiting for transfers between devices, prefix(): gathered = jax.tree.map(lambda a: lax.all_gather(a, axis), part)  328 us
    unnamed x1, blocking collectives  151 us
    psum x1, waiting for transfers between devices, body(): lax.psum((averaging_scale * jnp.dot(layer_input_rows.astype(jnp.float32)....  149 us
    add x63, other arithmetic, chain_step(): jnp.exp(later_part[0])[:, None, None] * earlier[1] + later_part[1]  74.8 us
    exp x63, local copies, waits for them, and re-layouts, chain_step(): jnp.exp(later_part[0])[:, None, None] * earlier[1] + later_part[1]  44 us
    psum x1, blocking collectives, body(): reverse_in_grad = lax.psum(back_part, 'head')  21.9 us
    psum x1, blocking collectives, body(): lax.psum(jnp.dot(output_gradient, adapter_up_out.T, preferred_element_typ...  21.8 us
  transfers between devices with their start and end apart: 7, of which 4 were waited for; matrix products, arithmetic and copies ran while one was open for 18% of the time, Pallas kernels for 0%

commit v1 on v0

--- a/solution.py
+++ b/solution.py
@@ -198,7 +198,11 @@
     back_part = jnp.dot(grad_conv, up_in_factor[0].T, precision=PRECISE_PRODUCT) + jnp.dot(
         grad_gate, up_in_factor[1].T, precision=PRECISE_PRODUCT
     )
-    reverse_in_grad = lax.psum(back_part, "head")
+    reverse_in_grad = back_part
+    for hop in (1, 2, 4):
+        reverse_in_grad = reverse_in_grad + lax.ppermute(
+            reverse_in_grad, "head", [(dev, dev ^ hop) for dev in range(8)]
+        )
     layer_gradient_fn = (
         ADAPTER_SCALE
         * jnp.dot(reverse_in_grad, adapter_down_in.astype(jnp.float32).T, precision=PRECISE_PRODUCT)

time: 907 us -> 945 us (1.042)
  waiting for transfers between devices: 481 us -> 500 us
    psum x1, waiting for transfers between devices: 149 us -> 163 us  [body(): lax.psum((averaging_scale * jnp.dot(layer_input_rows.astype(jnp.float32)....]
    psum x1, blocking collectives: 12.4 us -> 24.4 us  [body(): dot_total = lax.psum(jnp.sum(weighted * gated_out, axis=1), 'head')]
    psum x1, blocking collectives: 21.9 us -> 12.4 us  [body(): square_sum = lax.psum(square_part, 'head')]
  transfers between devices with their start and end apart: 7 -> 10, of which waited for: 4 -> 8; matrix products, arithmetic and copies ran while one was open for 18% -> 18% of each run, Pallas kernels for 0% -> 0%
where the time goes in v1:
time: 945 us; the launch traced here: 938 us
  waiting for transfers between devices  500 us (53%)
  blocking collectives  210 us (22%)
  other arithmetic  92.4 us (10%)
  local copies, waits for them, and re-layouts  64.2 us (7%)
  matrix products  40.7 us (4%)
  between operations  14.8 us (2%)
  starting transfers between devices  14.1 us (1%)
    all_gather x2, waiting for transfers between devices, prefix(): gathered = jax.tree.map(lambda a: lax.all_gather(a, axis), part)  326 us
    psum x1, waiting for transfers between devices, body(): lax.psum((averaging_scale * jnp.dot(layer_input_rows.astype(jnp.float32)....  163 us
    unnamed x1, blocking collectives  151 us
    add x63, other arithmetic, chain_step(): jnp.exp(later_part[0])[:, None, None] * earlier[1] + later_part[1]  74.8 us
    exp x63, local copies, waits for them, and re-layouts, chain_step(): jnp.exp(later_part[0])[:, None, None] * earlier[1] + later_part[1]  44 us
    psum x1, blocking collectives, body(): dot_total = lax.psum(jnp.sum(weighted * gated_out, axis=1), 'head')  24.4 us
    psum x1, blocking collectives, body(): lax.psum(jnp.dot(output_gradient, adapter_up_out.T, preferred_element_typ...  21.8 us
  transfers between devices with their start and end apart: 10, of which 8 were waited for; matrix products, arithmetic and copies ran while one was open for 18% of the time, Pallas kernels for 0%

profile of v1, /device:TPU:2, one launch (start us, length us, event | category | flops | bytes accessed | tf_op | source)
XLA Modules:
  0.0 938.1 jit_solution(5055806395263022290)
XLA Ops:
  8.1 4.3 collective-permute-start
  19.9 1.3 dynamic-slice
  22.1 151.3 %all-reduce.3 = f32[512]{0:T(512)S(1)} all-reduce(f32[512]{0:T(512)S(1)} %dynamic-update-slice), channel_id=2, replica_groups=mesh['seq'=64,'head'=8] {'seq'}, use_global_device_ids=true, to_apply=%add.3 | all-reduce | flops 512 | bytes 4096
  175.6 21.8 %psum.64 = f32[128,32]{0,1:T(8,128)} all-reduce(f32[128,32]{0,1:T(8,128)S(1)} %fusion.91), channel_id=1, replica_groups=mesh['seq'=64,'head'=8] {'head'}, use_global_device_ids=true, to_apply=%region_6.7 | all-reduce | flops 4096 | bytes 32768 | tf_op jit(solution)/shard_map/psum | solution.py:153
  198.3 1.7 fusion.92
  201.1 46.3 %all-gather.6.cloned.1.call-done = f32[512,128,128]{2,1,0:T(8,128)} async-done(((f32[8,128,128]{2,1,0:T(8,128)}), f32[512,128,128]{2,1,0:T(8,128)}) %all-gather.6.cloned.1.call-update) | async-done | bytes 33554448 | tf_op jit(solution)/shard_map/all_gather | solution.py:24
  248.1 1.3 convolution_bitcast_fusion.2
  249.4 2.1 fusion.6
  251.8 3.2 multiply_reduce_fusion.7
  254.9 12.4 %psum.63 = f32[128]{0:T(128)} all-reduce(f32[128]{0:T(128)} %get-tuple-element.523), channel_id=1, replica_groups=mesh['seq'=64,'head'=8] {'head'}, use_global_device_ids=true, to_apply=%region_5.6 | all-reduce | flops 128 | bytes 1024 | tf_op jit(solution)/shard_map/psum | solution.py:149
  268.5 1.9 fusion.41
  270.4 24.4 %all-reduce.5 = (f32[128]{0:T(128)}, f32[128,32]{0,1:T(8,128)}, f32[128,32]{0,1:T(8,128)}) all-reduce(f32[128]{0:T(128)} %get-tuple-element.524, f32[128,32]{0,1:T(8,128)} %fusion.92, f32[128,32]{0,1:T(8,128)} %fusion.41), channel_id=1, replica_groups=mesh['seq'=64,'head'=8] {'head'}, use_global_device_ids=true, to_apply=%region_8.9 | all-reduce | flops 8320 | bytes 66560 | tf_op jit(solution)/shard_map/psum | solution.py:160
  295.5 2.8 fusion.83
  298.4 1.2 copy.139
  299.6 1.9 convolution_bitcast_fusion.1
  301.5 2.0 copy.140
  303.7 1.3 broadcast_bitcast_fusion
  305.0 1.6 convolution_bitcast_fusion.9
  306.6 1.8 convolution_bitcast_fusion.6
  308.3 1.7 convolution_bitcast_fusion.8
  310.7 2.6 fusion.43
  313.3 1.5 convolution_multiply_fusion.3
  315.6 2.2 convolution_multiply_fusion.2
  317.9 280.0 %all-gather.8.cloned.1.call-done = f32[512,128,128]{2,1,0:T(8,128)} async-done(((f32[8,128,128]{2,1,0:T(8,128)}), f32[512,128,128]{2,1,0:T(8,128)}) %all-gather.8.cloned.1.call-update) | async-done | bytes 33554448 | tf_op jit(solution)/shard_map/all_gather | solution.py:24
  598.0 120.5 %while.21 = (s32[]{:T(128)}, f32[8,128,128]{2,1,0:T(8,128)S(1)}, s32[]{:T(128)}, f32[64,8]{1,0:T(8,128)}, f32[64,8,128,128]{3,2,1,0:T(8,128)}, /*index=5*/s32[]{:T(128)}, s32[]{:T(128)}, s32[]{:T(128)}, s32[]{:T(128)}) while((s32[]{:T(128)}, f32[8,128,128]{2,1,0:T(8,128)S(1)}, s32[]{:T(128)}, f32[64,8]{1,0:T(8,128)}, ...), condition=%wide.region_10.11_spmd, body=%wide.region_9.10_spmd.sunk | while | flops 262150 | bytes 1573115 | solution.py:33
  718.5 1.7 convolution_bitcast_fusion.10
  720.2 1.2 multiply_reduce_fusion.3
  721.4 1.7 convolution_add_fusion.2
  723.1 1.6 fusion.2
  724.9 1.4 add_multiply_fusion
  726.3 1.3 collective-permute-start.1
  728.0 4.0 collective-permute-done.1
  731.9 1.7 fusion.85
  733.6 1.2 fusion.65
  734.8 1.2 convolution_add_fusion.3
  736.1 1.9 collective-permute-start.2
  739.2 2.5 collective-permute-start.3
  742.7 2.1 collective-permute-done.3
  744.8 4.0 collective-permute-start.4
  748.8 1.6 maximum_multiply_fusion
  750.4 1.5 collective-permute-done.4
  757.6 1.7 fusion.7
  759.3 3.4 reduce-scatter.3.cloned.1.call-done
  762.7 162.7 %all-reduce.8.cloned.1.call-done = (f32[512,32]{0,1:T(8,128)}, f32[2,32,1024]{2,1,0:T(8,128)}, f32[1024,32]{0,1:T(8,128)}, f32[32,512]{1,0:T(8,128)}) async-done(((f32[512,32]{0,1:T(8,128)}, f32[2,32,1024]{2,1,0:T(8,128)}, f32[1024,32]{0,1:T(8,128)}, f32[32,512]{1,0:T(8,128)}), (f32[512,32]{0,1:T(8,128)}, f32[2,32,1024]{2,1,0:T(8,128)}, f32[1024,32]{0,1:T(8,128)}, ...) | async-done | bytes 524304 | tf_op jit(solution)/shard_map/psum | solution.py:211
  925.4 1.5 copy.191
  926.9 1.7 copy.192
  928.6 1.6 copy.193
  930.1 1.5 copy.194
  (224 shorter events, 144.4 us)
Async XLA Ops:
  7.2 167.5 %copy-start = (bf16[128,512]{1,0:T(8,128)(2,1)S(1)}, bf16[128,512]{1,0:T(8,128)(2,1)}, u32[]{:S(2)}) copy-start(bf16[128,512]{1,0:T(8,128)(2,1)} %param.32) | copy-start | bytes 393220
  7.2 307.7 %copy-start.4 = (bf16[128,128]{1,0:T(8,128)(2,1)S(1)}, bf16[128,128]{1,0:T(8,128)(2,1)}, u32[]{:S(2)}) copy-start(bf16[128,128]{1,0:T(8,128)(2,1)} %param.22) | copy-start | bytes 98308
  7.2 714.2 %copy-start.3 = (bf16[128,128]{1,0:T(8,128)(2,1)S(1)}, bf16[128,128]{1,0:T(8,128)(2,1)}, u32[]{:S(2)}) copy-start(bf16[128,128]{1,0:T(8,128)(2,1)} %param.23) | copy-start | bytes 98308
  7.2 744.7 %copy-start.5 = (bf16[128,512]{1,0:T(8,128)(2,1)S(1)}, bf16[128,512]{1,0:T(8,128)(2,1)}, u32[]{:S(2)}) copy-start(bf16[128,512]{1,0:T(8,128)(2,1)} %param.19) | copy-start | bytes 393220
  7.2 240.2 %all-gather.6.cloned.1.call-start = ((), (), s32[]{:S(2)}) async-start(), calls=%async_computation.4 | async-start | bytes 34078720 | tf_op jit(solution)/shard_map/all_gather | solution.py:24
  8.1 6.5 collective-permute-start
  13.2 3.5 copy-start.11
  13.2 3.5 copy-start.12
  13.2 3.5 copy-start.13
  13.2 3.5 copy-start.14
  14.2 159.3 %copy-start.10 = (f32[128,8]{0,1:T(8,128)}, f32[128,8]{0,1:T(8,128)S(1)}, u32[]{:S(2)}) copy-start(f32[128,8]{0,1:T(8,128)S(1)} %copy.132) | copy-start | bytes 12292
  14.5 182.8 %copy-start.7 = (f32[128,8]{0,1:T(8,128)}, f32[128,8]{0,1:T(8,128)S(1)}, u32[]{:S(2)}) copy-start(f32[128,8]{0,1:T(8,128)S(1)} %get-tuple-element.571) | copy-start | bytes 12292
  14.5 237.0 %copy-start.9 = (f32[128,8]{0,1:T(8,128)}, f32[128,8]{0,1:T(8,128)S(1)}, u32[]{:S(2)}) copy-start(f32[128,8]{0,1:T(8,128)S(1)} %get-tuple-element.572) | copy-start | bytes 12292
  19.1 578.8 %all-gather.8.cloned.1.call-start = ((), (), s32[]{:S(2)}) async-start(), calls=%async_computation.5 | async-start | bytes 34078720 | tf_op jit(solution)/shard_map/all_gather | solution.py:24
  173.6 78.0 %copy-start.8 = (f32[8,128]{1,0:T(8,128)}, f32[8,128]{1,0:T(8,128)S(1)}, u32[]{:S(2)}) copy-start(f32[8,128]{1,0:T(8,128)S(1)} %copy.129) | copy-start | bytes 12292
  247.5 0.6 copy-start.15
  251.7 43.8 %copy-start.2 = (f32[128,1024]{1,0:T(8,128)}, f32[128,1024]{1,0:T(8,128)S(1)}, u32[]{:S(2)}) copy-start(f32[128,1024]{1,0:T(8,128)S(1)} %copy.138) | copy-start | bytes 1572868
  254.9 43.4 %copy-start.1 = (f32[128,1024]{1,0:T(8,128)}, f32[128,1024]{1,0:T(8,128)S(1)}, u32[]{:S(2)}) copy-start(f32[128,1024]{1,0:T(8,128)S(1)} %get-tuple-element.558) | copy-start | bytes 1572868
  267.9 0.5 copy-start.16
  303.6 455.7 %reduce-scatter.5.cloned.1.call-start = ((), (), s32[]{:S(2)}) async-start(), calls=%async_computation.3 | async-start | bytes 73728 | tf_op jit(solution)/shard_map/reduce_scatter | solution.py:192
  313.3 284.6 %copy-start.6 = (f32[128,128]{1,0:T(8,128)}, f32[128,128]{1,0:T(8,128)S(1)}, u32[]{:S(2)}) copy-start(f32[128,128]{1,0:T(8,128)S(1)} %get-tuple-element.518) | copy-start | bytes 196612
  317.9 444.9 %reduce-scatter.3.cloned.1.call-start = ((), (), s32[]{:S(2)}) async-start(), calls=%async_computation.2 | async-start | bytes 73728 | tf_op jit(solution)/shard_map/reduce_scatter | solution.py:191
  726.3 5.6 collective-permute-start.1
  736.1 3.1 collective-permute-start.2
  738.8 186.6 %all-reduce.8.cloned.1.call-start = ((), (), s32[]{:S(2)}) async-start(), calls=%async_computation.6 | async-start | bytes 1048576 | tf_op jit(solution)/shard_map/psum | solution.py:211
  739.2 5.6 collective-permute-start.3
  744.8 7.1 collective-permute-start.4
Sparse Core Ops, SparseCore 0:
  19.2 228.1 all-gather.5
  303.7 294.1 all-gather.7
  601.3 30.7 reduce-scatter.4
  738.9 23.7 reduce-scatter.2
  767.4 158.0 all-reduce.7
